TPU v7x, 32 devices: a whole 2x2x4 slice. The times are simulated.
32 devices in a mesh: outer: 4 (over y, core), row: 4 (over z), col: 2 (over x).
Axes of the slice: x: 2, y: 2, z: 4, core: 2. Of those that a mesh axis runs over, the one named last changes fastest.
Arguments:
- activations: bfloat16 [2048, 9216], P(('outer', 'col'), 'row'), may hold values from -13 to 13
- out_grads: bfloat16 [2048, 8192], P(('outer', 'row'), 'col'), may hold values from -13 to 13
- row_moment: float32 [9216], P(('row', 'outer')), may hold values from 0.3 to 3
- col_moment: float32 [8192], P('col'), may hold values from 0.3 to 3
Outputs:
- update: bfloat16 [9216, 8192], P(('row', 'outer'), 'col')
- new_row: float32 [9216], P(('row', 'outer'))
- new_col: float32 [8192], P('col')
All inputs are finite; a program needn't handle non-finite values.
Results may differ from a plain program's by a relative error of at most 0.001.
Values may be sent and summed in bfloat16 or wider, within the bound.
A program may use at most 128 MiB of HBM per device.

v0:
```python
import functools

import jax
import jax.numpy as jnp
from jax import lax
from jax.experimental import pallas as pl
from jax.experimental.pallas import tpu as pltpu
from jax.sharding import PartitionSpec as P

D = 9216
F = 8192
STEP = 2
MESH = pl.DeviceIdType.MESH
PIECES = 4
BY_Y = 1


def kernel(
    nout, nz, ncol, scale, decay,
    raw_ref, g_ref, rm_hbm, cm_hbm,
    acc, nr_ref, nrc_ref, nc_ref, mt_ref,
    gs, av, raw, a_ref, rm_ref, cm_ref, rowp, colbuf, colz, rowbuf, totz, toto,
    g_recv, zp_send, zm_send, y_send, p_send, a_recv, a1_send, a2_send, loc_sem,
    c_send, c_recv, cz_send, cz_recv, r_send, r_recv, tz_send, tz_recv, to_send, to_recv,
):
    tg, width = g_ref.shape
    rows, ta = av.shape[1], av.shape[2]
    piece = width // PIECES
    o = lax.axis_index("outer")
    z = lax.axis_index("row")
    x = lax.axis_index("col")
    y, core = o // 2, o % 2
    oy = (1 - y) * 2 + core
    op = y * 2 + (1 - core)
    mate = z + 1 - 2 * (z % 2)

    def remote(src, dst, s, r, dev):
        return pltpu.make_async_remote_copy(
            src_ref=src, dst_ref=dst, send_sem=s, recv_sem=r, device_id=dev, device_id_type=MESH
        )

    load_a = pltpu.make_async_copy(raw_ref, raw, loc_sem.at[2])
    load_a.start()
    load_rm = pltpu.make_async_copy(rm_hbm, rm_ref, loc_sem.at[3])
    load_cm = pltpu.make_async_copy(cm_hbm, cm_ref, loc_sem.at[4])
    load_rm.start()
    load_cm.start()
    barrier = pltpu.get_barrier_semaphore()
    for d in range(1, nout):
        pl.semaphore_signal(barrier, inc=1, device_id={"outer": (o + d) % nout}, device_id_type=MESH)

    @pl.when(z > 0)
    def _():
        pl.semaphore_signal(barrier, inc=1, device_id={"row": jnp.maximum(z - 1, 0)}, device_id_type=MESH)

    @pl.when(z < nz - 1)
    def _():
        pl.semaphore_signal(barrier, inc=1, device_id={"row": jnp.minimum(z + 1, nz - 1)}, device_id_type=MESH)

    for d in range(1, ncol):
        pl.semaphore_signal(barrier, inc=1, device_id={"col": (x + d) % ncol}, device_id_type=MESH)
    ends = jnp.where(z > 0, 1, 0) + jnp.where(z < nz - 1, 1, 0)
    pl.semaphore_wait(barrier, nout + ncol - 2 + ends)

    def slot(oo, zz):
        return oo * nz + zz

    def place(s, h):
        return gs.at[pl.ds(pl.multiple_of(s * tg, tg), tg), pl.ds(h * piece, piece)]

    def g_copy(src, s, h, sem, dev):
        return remote(src, place(s, h), sem, g_recv.at[s, h], dev)

    def to_up(src, oo, zz, h):
        k = jnp.where(oo == o, zz, nz)
        return g_copy(src, slot(oo, zz), h, zp_send.at[k, h], {"row": jnp.minimum(z + 1, nz - 1)})

    def to_down(src, oo, zz, h):
        k = jnp.where(oo == o, zz, nz)
        return g_copy(src, slot(oo, zz), h, zm_send.at[k, h], {"row": jnp.maximum(z - 1, 0)})

    def to_y(src, zz, h):
        return g_copy(src, slot(o, zz), h, y_send.at[zz, h], {"outer": oy})

    def to_partner(src, oo, zz, h):
        k = jnp.where(oo == o, zz, nz + zz)
        return g_copy(src, slot(oo, zz), h, p_send.at[k, h], {"outer": op})

    def arrived(oo, zz, h):
        here = place(slot(oo, zz), h)
        to_partner(here, oo, zz, h).wait_recv()
        return here

    own = [g_ref.at[:, pl.ds(h * piece, piece)] for h in range(PIECES)]
    for h in range(PIECES):
        @pl.when(z < nz - 1)
        def _():
            to_up(own[h], o, z, h).start()

        @pl.when(z > 0)
        def _():
            to_down(own[h], o, z, h).start()

        to_y(own[h], z, h).start()
        to_partner(own[h], o, z, h).start()

    def a_first(d):
        target = (o + d) % nout
        return remote(a_ref.at[target], av.at[o * ncol + x], a1_send.at[d], a_recv.at[o * ncol + x], {"outer": target})

    def a_second(oo, d, own=False):
        k = oo * ncol + x
        src = a_ref.at[o] if own else av.at[k]
        return remote(src, av.at[k], a2_send.at[oo, d], a_recv.at[k], {"col": (x + d) % ncol})

    local_g = pltpu.make_async_copy(g_ref, gs.at[pl.ds(pl.multiple_of(slot(o, z) * tg, tg), tg), :], loc_sem.at[0])
    local_a = pltpu.make_async_copy(a_ref.at[o], av.at[o * ncol + x], loc_sem.at[1])
    local_g.start()
    load_a.wait()
    turned = jnp.transpose(raw[...])
    for k in range(nout):
        a_ref[k] = turned[k * rows : (k + 1) * rows]

    def a_arrived(k):
        remote(av.at[k], av.at[k], a1_send.at[1], a_recv.at[k], {"outer": oy}).wait_recv()

    def pass_on(oo):
        a_arrived(oo * ncol + x)
        for d in range(1, ncol):
            a_second(oo, d).start()

    def y_arrived(zz):
        for h in range(PIECES):
            here = arrived(oy, zz, h)
            to_partner(here, oy, zz, h).start()

    def extra(h, act):
        here = place(slot(oy, z), h)

        @pl.when(mate > z)
        def _():
            act(to_up(here, oy, z, h))

        @pl.when(mate < z)
        def _():
            act(to_down(here, oy, z, h))

    for s in range(1, nz):
        for h in range(PIECES):
            @pl.when(z - s >= 0)
            def _():
                here = arrived(o, z - s, h)

                @pl.when(z < nz - 1)
                def _():
                    to_up(here, o, z - s, h).start()

                @pl.when((z - s != mate) | (h < BY_Y))
                def _():
                    to_y(here, z - s, h).start()

                to_partner(here, o, z - s, h).start()

            @pl.when(z + s < nz)
            def _():
                here = arrived(o, z + s, h)

                @pl.when(z > 0)
                def _():
                    to_down(here, o, z + s, h).start()

                @pl.when((z + s != mate) | (h < BY_Y))
                def _():
                    to_y(here, z + s, h).start()

                to_partner(here, o, z + s, h).start()

            if s == 1 and h == 0:
                for d in range(1, nout):
                    a_first(d).start()
                for d in range(1, ncol):
                    a_second(o, d, True).start()
                local_a.start()

        if s == 1:
            y_arrived(z)
            pass_on(op)
        if s == min(2, nz - 1):
            for c in range(2):
                pass_on((1 - y) * 2 + c)
        if 1 < s < nz - 1:
            for zz in (z - (s - 1), z + (s - 1)):
                @pl.when((zz >= 0) & (zz < nz) & (zz != mate))
                def _():
                    y_arrived(zz)
        if s == max(nz - 2, 1):
            for h in range(BY_Y, PIECES):
                extra(h, lambda c: c.start())

    local_g.wait()
    local_a.wait()
    load_rm.wait()
    load_cm.wait()
    for d in range(1, ncol):
        for q in range(nout):
            a_arrived(((o + q) % nout) * ncol + (x + d) % ncol)
    for zz in range(nz):
        for h in range(PIECES):
            arrived(op, zz, h)
    tile = min(512, piece)
    per_piece = piece // tile

    def dots(yy, columns):
        total = None
        for k in range(2 * ncol):
            block = yy * 2 * ncol + k
            part = jnp.dot(
                av[block],
                gs[pl.ds(pl.multiple_of(block * ta, ta), ta), columns],
                preferred_element_type=jnp.float32,
            )
            total = part if total is None else total + part
        return total

    @pl.loop(0, width // tile)
    def _(j):
        columns = pl.ds(pl.multiple_of(j * tile, tile), tile)
        acc[:, columns] = dots(y, columns)

    rowp[...] = jnp.zeros_like(rowp)
    od = (1 - y) * 2 + (1 - core)
    def finish_piece(h):
        for zz in range(nz):
            arrived(od, zz, h)

        @pl.loop(h * per_piece, (h + 1) * per_piece)
        def _(j):
            columns = pl.ds(pl.multiple_of(j * tile, tile), tile)
            grad = (acc[:, columns] + dots(1 - y, columns)) * scale
            acc[:, columns] = grad
            squares = grad * grad
            part = squares[:, :128]
            for i in range(1, tile // 128):
                part = part + squares[:, i * 128 : (i + 1) * 128]
            rowp[...] += part
            colbuf[0, :, columns] = jnp.sum(squares, axis=0, keepdims=True)

    for h in range(PIECES):
        for s in range(nz - 2, nz):
            if s > 1 or (s == 1 and nz == 2):
                for zz in (z - s, z + s):
                    @pl.when((zz >= 0) & (zz < nz) & (zz != mate))
                    def _():
                        here = arrived(oy, zz, h)
                        to_partner(here, oy, zz, h).start()

        here = arrived(oy, mate, h)
        to_partner(here, oy, mate, h).start()
        if h > 0:
            finish_piece(h - 1)
    finish_piece(PIECES - 1)

    def c_first(d):
        return remote(colbuf.at[0], colbuf.at[nout - d], c_send.at[d], c_recv.at[nout - d], {"outer": (o + d) % nout})

    def c_second(d):
        return remote(colz.at[0], colz.at[nz - d], cz_send.at[d], cz_recv.at[nz - d], {"row": (z + d) % nz})

    def r_first(d):
        return remote(rowbuf.at[0], rowbuf.at[ncol - d], r_send.at[d], r_recv.at[ncol - d], {"col": (x + d) % ncol})

    def t_first(d):
        return remote(toto.at[0], toto.at[nout - d], to_send.at[d], to_recv.at[nout - d], {"outer": (o + d) % nout})

    def t_second(d, e):
        k = ((nz - d) % nz) * ncol + (ncol - e) % ncol
        dev = {"row": (z + d) % nz, "col": (x + e) % ncol}
        return remote(totz.at[0], totz.at[k], tz_send.at[d * ncol + e], tz_recv.at[k], dev)

    def finish(copies):
        for c in copies:
            c.wait()

    firsts = [c_first(d) for d in range(1, nout)]
    for c in firsts:
        c.start()
    mine = jnp.sum(jnp.transpose(rowp[...]), axis=0, keepdims=True)
    rowbuf[0] = mine
    rights = [r_first(d) for d in range(1, ncol)]
    for c in rights:
        c.start()
    share = (decay / ncol) * rm_ref[...].reshape(1, rows) + ((1.0 - decay) / F) * mine
    toto[0] = jnp.broadcast_to(jnp.sum(share, axis=1, keepdims=True), toto.shape[1:])
    tots = [t_first(d) for d in range(1, nout)]
    for c in tots:
        c.start()
    finish(firsts)
    col_sq = colbuf[0]
    for d in range(1, nout):
        col_sq = col_sq + colbuf[d]
    colz[0] = col_sq
    finish(rights)
    seconds = [c_second(d) for d in range(1, nz)]
    for c in seconds:
        c.start()
    finish(tots)
    total = toto[0]
    for d in range(1, nout):
        total = total + toto[d]
    totz[0] = total
    lasts = [t_second(d, e) for d in range(nz) for e in range(ncol) if d + e > 0]
    for c in lasts:
        c.start()
    row_sq = rowbuf[0]
    for d in range(1, ncol):
        row_sq = row_sq + rowbuf[d]
    new_row = decay * rm_ref[...].reshape(1, rows) + (1.0 - decay) * row_sq / F
    nr_ref[...] = new_row
    nrc_ref[...] = jnp.transpose(jnp.broadcast_to(new_row, (128, new_row.shape[1])))
    finish(seconds)
    col_sq = colz[0]
    for d in range(1, nz):
        col_sq = col_sq + colz[d]
    nc_ref[...] = decay * cm_ref[...].reshape(1, width) + (1.0 - decay) * col_sq / D
    finish(lasts)
    total = totz[0]
    for k in range(1, nz * ncol):
        total = total + totz[k]
    mt_ref[...] = total

    for h in range(PIECES):
        for zz in range(nz):
            @pl.when((z < nz - 1) & (zz <= z))
            def _():
                to_up(place(slot(o, zz), h), o, zz, h).wait_send()

            @pl.when((z > 0) & (zz >= z))
            def _():
                to_down(place(slot(o, zz), h), o, zz, h).wait_send()

            @pl.when((zz != mate) | (h < BY_Y))
            def _():
                to_y(place(slot(o, zz), h), zz, h).wait_send()

            to_partner(place(slot(o, zz), h), o, zz, h).wait_send()
            to_partner(place(slot(oy, zz), h), oy, zz, h).wait_send()
        if h >= BY_Y:
            extra(h, lambda c: c.wait_send())
    for d in range(1, nout):
        a_first(d).wait_send()
    for oo in range(nout):
        for d in range(1, ncol):
            a_second(oo, d).wait_send()


def update_kernel(step, grad_ref, nr_ref, nc_ref, mt_ref, flat_ref, out_ref, row_ref, col_ref):
    here = pl.ds(pl.multiple_of(pl.program_id(0) * step, step), step)
    scale = D / mt_ref[0, 0]
    by_row = lax.rsqrt(nr_ref[here, :1])
    by_col = lax.rsqrt(nc_ref[...] * scale)
    @pl.when(pl.program_id(0) == 0)
    def _():
        row_ref[...] = flat_ref[...].reshape(row_ref.shape)
        col_ref[...] = nc_ref[...].reshape(col_ref.shape)

    out_ref[...] = (grad_ref[here, :] * by_row * by_col).astype(out_ref.dtype)


def body(nout, nz, ncol, activations, out_grads, row_moment, col_moment):
    rows, width = row_moment.shape[0], col_moment.shape[0]
    ta, tg = activations.shape[0], out_grads.shape[0]
    tokens = ta * ncol * nout
    decay = 1.0 - STEP ** (-0.8)
    f32, bf16 = jnp.float32, jnp.bfloat16
    vmem = pl.BlockSpec(memory_space=pltpu.VMEM)
    dma = pltpu.SemaphoreType.DMA
    grad, new_row, turned_row, new_col, total = pl.pallas_call(
        functools.partial(kernel, nout, nz, ncol, 1.0 / tokens**0.5, decay),
        out_shape=(
            pltpu.VMEM((rows, width), f32),
            jax.ShapeDtypeStruct((1, rows), f32),
            pltpu.VMEM((rows, 128), f32),
            jax.ShapeDtypeStruct((1, width), f32),
            jax.ShapeDtypeStruct((1, 128), f32),
        ),
        in_specs=[pl.BlockSpec(memory_space=pl.ANY)] * 4,
        out_specs=(vmem,) * 5,
        scratch_shapes=[
            pltpu.VMEM((tokens, width), bf16),
            pltpu.VMEM((nout * ncol, rows, ta), bf16),
            pltpu.VMEM(activations.shape, bf16),
            pltpu.VMEM((nout, rows, ta), bf16),
            pltpu.VMEM((rows,), f32),
            pltpu.VMEM((width,), f32),
            pltpu.VMEM((rows, 128), f32),
            pltpu.VMEM((nout, 1, width), f32),
            pltpu.VMEM((nz, 1, width), f32),
            pltpu.VMEM((ncol, 1, rows), f32),
            pltpu.VMEM((nz * ncol, 1, 128), f32),
            pltpu.VMEM((nout, 1, 128), f32),
            dma((nout * nz, PIECES)),
            dma((nz + 1, PIECES)),
            dma((nz + 1, PIECES)),
            dma((nz, PIECES)),
            dma((2 * nz, PIECES)),
            dma((nout * ncol,)),
            dma((nout,)),
            dma((nout, ncol)),
            dma((5,)),
            dma((nout,)), dma((nout,)),
            dma((nz,)), dma((nz,)),
            dma((ncol,)), dma((ncol,)),
            dma((nz * ncol,)), dma((nz * ncol,)),
            dma((nout,)), dma((nout,)),
        ],
        compiler_params=pltpu.CompilerParams(
            collective_id=0, has_side_effects=True, vmem_limit_bytes=44 * 1024 * 1024
        ),
    )(activations, out_grads, row_moment, col_moment)
    parts = next(n for n in (4, 3, 2, 1) if n == 1 or rows % (n * 16) == 0)
    step = rows // parts
    update, flat_row, flat_col = pl.pallas_call(
        functools.partial(update_kernel, step),
        grid=(parts,),
        out_shape=(
            jax.ShapeDtypeStruct((rows, width), bf16),
            jax.ShapeDtypeStruct((rows,), f32),
            jax.ShapeDtypeStruct((width,), f32),
        ),
        in_specs=[vmem] * 5,
        out_specs=(pl.BlockSpec((step, width), lambda i: (i, 0)), vmem, vmem),
        compiler_params=pltpu.CompilerParams(vmem_limit_bytes=24 * 1024 * 1024),
    )(grad, turned_row, new_col, total, new_row)
    return (update, flat_row, flat_col)


def solution(mesh):
    nout, nz, ncol = mesh.shape["outer"], mesh.shape["row"], mesh.shape["col"]
    return jax.shard_map(
        functools.partial(body, nout, nz, ncol),
        mesh=mesh,
        in_specs=(
            P(("outer", "col"), "row"),
            P(("outer", "row"), "col"),
            P(("row", "outer")),
            P("col"),
        ),
        out_specs=(P(("row", "outer"), "col"), P(("row", "outer")), P("col")),
        check_vma=False,
    )
```

profile of v0, /device:TPU:0, one launch (start us, length us, event | category | flops | bytes accessed | tf_op | source)
XLA Modules:
  0.0 111.0 jit_solution(3029757928029688957)
XLA Ops:
  0.6 0.0 copy-start
  0.6 0.7 copy-done
  1.3 0.0 copy-start.1
  1.4 0.7 copy-done.1
  2.0 105.8 %shard_map.67 = (f32[576,4096]{1,0:T(8,128)S(1)}, f32[1,576]{1,0:T(1,128)S(1)}, f32[576,128]{1,0:T(8,128)S(1)}, f32[1,4096]{1,0:T(1,128)S(1)}, f32[1,128]{1,0:T(1,128)S(1)}) custom-call(bf16[256,2304]{1,0:T(8,128)(2,1)} %raw_ref.1, bf16[128,4096]{1,0:T(8,128)(2,1)} %g_ref.1, f32[576]{0:T(1024)S(1)} %copy-done.1, f32[4096]{0:T(1024)S(1)} %copy-done), custom_call_target="tpu_custom_call" | custom-call | tf_op jit(solution)/shard_map/pallas_call | solution.py:377
  107.8 3.2 %shard_map.68 = (bf16[576,4096]{1,0:T(8,128)(2,1)}, f32[576]{0:T(1024)}, f32[4096]{0:T(1024)}) custom-call(f32[576,4096]{1,0:T(8,128)S(1)} %get-tuple-element.8.grad_ref, f32[576,128]{1,0:T(8,128)S(1)} %get-tuple-element.9.nr_ref, f32[1,4096]{1,0:T(1,128)S(1)} %get-tuple-element.10.nc_ref, f32[1,128]{1,0:T(1,128)S(1)} %get-tuple-element.11.mt_ref, ...), custom_call_target="tpu_custom_call" | custom-call | tf_op jit(solution)/shard_map/pallas_call | solution.py:422
Async XLA Ops:
  0.6 0.7 copy-start
  1.3 0.7 copy-start.1
where the time goes:
time: 111 us
  Pallas kernels  109 us (98%)
  local copies, waits for them, and re-layouts  1.4 us (1%)
    pallas_call x1, Pallas kernels, body(): pl.pallas_call(functools.partial(kernel, nout, nz, ncol, 1.0 / tokens **...  106 us
    pallas_call x1, Pallas kernels, body(): pl.pallas_call(functools.partial(update_kernel, step), grid=(parts,), out...  3.18 us

commit v1 on v0

v1 whole, which is shorter than its diff:
```python
import functools

import jax
import jax.numpy as jnp
from jax import lax
from jax.experimental import pallas as pl
from jax.experimental.pallas import tpu as pltpu
from jax.sharding import PartitionSpec as P

D = 9216
F = 8192
STEP = 2
MESH = pl.DeviceIdType.MESH


def cuts(width):
    unit = width // 128
    share, *edges = [round(unit * e / 32) * 128 for e in (7, 16, 24, 28, 32)]
    fine = [(a, b - a) for a, b in zip([0] + edges[:-1], edges)]
    chain = [[0], [1], [2, 3]]
    by_y = (0, share)
    by_z = [(share, edges[0] - share)] + fine[1:]
    return fine, chain, by_y, by_z


def each(first, last, f):
    if last - first <= 32:
        for k in range(first, last):
            f(k)
    else:
        pl.loop(first, last)(f)


def kernel(
    nout, nz, ncol, scale, decay,
    raw_ref, g_ref, rm_hbm, cm_hbm,
    acc, nr_ref, byrow_ref, nc_ref, bycol_ref,
    gs, av, raw, a_ref, rm_ref, cm_ref, rowp, early, earlyz, late, others, rowbuf,
    gz_recv, gy_recv, op_recv, od_recv, a1_recv, a2_recv,
    zp_send, zm_send, x_send, y_send, p_send, a1_send, a2_send, loc_sem,
    e_sem, ez_sem, l_sem, o_sem, r_sem, ready,
):
    tg, width = g_ref.shape
    rows, ta = av.shape[1], av.shape[2]
    fine, chain, by_y, by_z = cuts(width)
    last = len(fine) - 1
    wide = early.shape[2]
    o = lax.axis_index("outer")
    z = lax.axis_index("row")
    x = lax.axis_index("col")
    y, core = o // 2, o % 2
    oy = (1 - y) * 2 + core
    op = y * 2 + (1 - core)
    od = (1 - y) * 2 + (1 - core)
    mate = z + 1 - 2 * (z % 2)
    up = {"row": jnp.minimum(z + 1, nz - 1)}
    down = {"row": jnp.maximum(z - 1, 0)}

    def remote(src, dst, s, r, dev):
        return pltpu.make_async_remote_copy(
            src_ref=src, dst_ref=dst, send_sem=s, recv_sem=r, device_id=dev, device_id_type=MESH
        )

    def settle(ref, sem):
        pltpu.make_async_copy(ref, ref, sem).wait()

    load_a = pltpu.make_async_copy(raw_ref, raw, loc_sem.at[2])
    load_a.start()
    load_rm = pltpu.make_async_copy(rm_hbm, rm_ref, loc_sem.at[3])
    load_cm = pltpu.make_async_copy(cm_hbm, cm_ref, loc_sem.at[4])
    load_rm.start()
    load_cm.start()
    barrier = pltpu.get_barrier_semaphore()
    for d in range(1, nout):
        pl.semaphore_signal(barrier, inc=1, device_id={"outer": (o + d) % nout}, device_id_type=MESH)

    @pl.when(z > 0)
    def _():
        pl.semaphore_signal(barrier, inc=1, device_id=down, device_id_type=MESH)

    @pl.when(z < nz - 1)
    def _():
        pl.semaphore_signal(barrier, inc=1, device_id=up, device_id_type=MESH)

    for d in range(1, ncol):
        pl.semaphore_signal(barrier, inc=1, device_id={"col": (x + d) % ncol}, device_id_type=MESH)
    ends = jnp.where(z > 0, 1, 0) + jnp.where(z < nz - 1, 1, 0)
    pl.semaphore_wait(barrier, nout + ncol - 2 + ends)

    def slots(oo, zz, count, cols):
        start = pl.multiple_of((oo * nz + zz) * tg, tg)
        return gs.at[pl.ds(start, count * tg), pl.ds(*cols)]

    def place(oo, zz, cols):
        return slots(oo, zz, 1, cols)

    def merged(c):
        first, end = fine[chain[c][0]], fine[chain[c][-1]]
        return (first[0], end[0] + end[1] - first[0])

    full = (0, width)

    def to_up(src, zz, c):
        return remote(src, place(o, zz, merged(c)), zp_send, gz_recv.at[zz, c], up)

    def to_down(src, zz, c):
        return remote(src, place(o, zz, merged(c)), zm_send, gz_recv.at[zz, c], down)

    def to_y(src, zz, cols, j, sem):
        return remote(src, place(o, zz, cols), sem, gy_recv.at[zz, j], {"outer": oy})

    def near(src, zz, c):
        return remote(src, place(o, zz, merged(c)), p_send, op_recv.at[c], {"outer": op})

    def far(zz, cols, h):
        here = place(oy, zz, cols)
        return remote(here, here, p_send, od_recv.at[h], {"outer": op})

    for c in range(len(chain)):
        own = g_ref.at[:, pl.ds(*merged(c))]

        @pl.when(z < nz - 1)
        def _():
            to_up(own, z, c).start()

        @pl.when(z > 0)
        def _():
            to_down(own, z, c).start()

        if c == 0:
            to_y(g_ref, z, full, 0, y_send.at[0]).start()
        near(own, z, c).start()

    def a_first(d):
        target = (o + d) % nout
        return remote(a_ref.at[target], av.at[o * ncol + x], a1_send, a1_recv.at[o], {"outer": target})

    def a_second(oo, d, own=False):
        k = oo * ncol + x
        return remote(a_ref.at[o] if own else av.at[k], av.at[k], a2_send, a2_recv, {"col": (x + d) % ncol})

    local_g = pltpu.make_async_copy(g_ref, slots(o, z, 1, full), loc_sem.at[0])
    local_a = pltpu.make_async_copy(a_ref.at[o], av.at[o * ncol + x], loc_sem.at[1])
    local_g.start()
    load_a.wait()
    turned = jnp.transpose(raw[...])
    for k in range(nout):
        a_ref[k] = turned[k * rows : (k + 1) * rows]

    def pass_on(oo):
        k = oo * ncol + x
        remote(av.at[k], av.at[k], a1_send, a1_recv.at[oo], {"outer": oy}).wait_recv()
        for d in range(1, ncol):
            a_second(oo, d).start()

    def landed(zz, cols, j):
        here = place(oy, zz, cols)
        remote(here, here, y_send.at[0], gy_recv.at[zz, j], {"outer": oy}).wait_recv()

    def take(zz, h):
        landed(zz, fine[h], h)
        far(zz, fine[h], h).start()

    def take_mate(h):
        if h == 0:
            landed(mate, by_y, 0)
            far(mate, by_y, 0).start()
        landed(mate, by_z[h], h + 1)
        far(mate, by_z[h], h).start()

    def relay(zz, c, onward):
        here = place(o, zz, merged(c))
        remote(here, here, zp_send, gz_recv.at[zz, c], up).wait_recv()
        onward(here)

        @pl.when(zz != mate)
        def _():
            for j in chain[c]:
                to_y(place(o, zz, fine[j]), zz, fine[j], j, y_send.at[0]).start()

        if c == 0:
            @pl.when(zz == mate)
            def _():
                to_y(place(o, zz, by_y), zz, by_y, 0, y_send.at[1]).start()

        near(here, zz, c).start()

    def extra(act):
        for h in range(len(fine)):
            here = place(oy, z, by_z[h])

            @pl.when(mate > z)
            def _():
                act(remote(here, here, x_send, gy_recv.at[z, h + 1], up))

            @pl.when(mate < z)
            def _():
                act(remote(here, here, x_send, gy_recv.at[z, h + 1], down))

    def dots(oo, cols):
        total = None
        for k in range(ncol):
            block = oo * ncol + k
            part = jnp.dot(
                av[block],
                gs[pl.ds(pl.multiple_of(block * ta, ta), ta), cols],
                preferred_element_type=jnp.float32,
            )
            total = part if total is None else total + part
        return total

    def tiles(cols, f):
        start, size = cols
        tile = 512 if size % 512 == 0 else size

        @pl.loop(0, size // tile)
        def _(j):
            f(pl.multiple_of(j * tile, 128), tile)

    def first_half(c):
        slots_here = slots(op, 0, nz, merged(c))
        remote(slots_here, slots_here, p_send, op_recv.at[c], {"outer": op}).wait_recv()
        base = merged(c)[0]

        def one(offset, tile):
            cols = pl.ds(pl.multiple_of(base + offset, 128), tile)
            acc[:, cols] = dots(o, cols) + dots(op, cols)

        tiles(merged(c), one)

    for s in range(1, nz):
        if s == nz - 1:
            local_g.wait()
            local_a.wait()
            settle(av.at[pl.ds(0, (ncol - 1) * nout)], a2_recv)
        for c in range(len(chain)):
            @pl.when(z - s >= 0)
            def _():
                def onward(here):
                    @pl.when(z < nz - 1)
                    def _():
                        to_up(here, z - s, c).start()

                relay(z - s, c, onward)

            @pl.when(z + s < nz)
            def _():
                def onward(here):
                    @pl.when(z > 0)
                    def _():
                        to_down(here, z + s, c).start()

                relay(z + s, c, onward)

            if s == 1 and c == 0:
                for d in range(1, nout):
                    a_first(d).start()
                for d in range(1, ncol):
                    a_second(o, d, True).start()
                local_a.start()
            if s == nz - 1:
                first_half(c)

        if s == 1:
            landed(z, full, 0)
            for h in range(len(fine)):
                far(z, fine[h], h).start()
            pass_on(op)
        if s == min(2, nz - 1):
            for c in range(2):
                pass_on((1 - y) * 2 + c)
        if s == max(nz - 2, 1):
            extra(lambda c: c.start())
        if 1 < s < nz - 1:
            for zz in (z - (s - 1), z + (s - 1)):
                @pl.when((zz >= 0) & (zz < nz) & (zz != mate))
                def _():
                    for h in range(len(fine)):
                        take(zz, h)

    rowp[...] = jnp.zeros_like(rowp)
    load_rm.wait()
    load_cm.wait()
    old = rm_ref[...].reshape(1, rows)
    old_share = jnp.broadcast_to(jnp.sum(old, axis=1, keepdims=True) * (decay / ncol / 128), (1, 128))

    def finish(h, split=False):
        begin, size = fine[h]
        sums, shift = (early, 0) if begin < wide else (late, wide)

        def od_wait():
            here = slots(od, 0, nz, fine[h])
            remote(here, here, p_send, od_recv.at[h], {"outer": op}).wait_recv()

        def one(offset, tile):
            cols = pl.ds(pl.multiple_of(begin + offset, 128), tile)
            there = pl.ds(pl.multiple_of(begin - shift + offset, 128), tile)
            grad = (acc[:, cols] + dots(od, cols)) * scale if split else (acc[:, cols] + (dots(oy, cols) + dots(od, cols))) * scale
            acc[:, cols] = grad
            squares = grad * grad
            part = squares[:, :128]
            for i in range(1, tile // 128):
                part = part + squares[:, i * 128 : (i + 1) * 128]
            rowp[...] += part
            sums[0, :, there] = jnp.sum(squares, axis=0, keepdims=True)

        def ahead(offset, tile):
            cols = pl.ds(pl.multiple_of(begin + offset, 128), tile)
            acc[:, cols] = acc[:, cols] + dots(oy, cols)

        if split:
            tiles(fine[h], ahead)
        od_wait()
        tiles(fine[h], one)

    def e_first(d):
        return remote(early.at[0], early.at[nout - d], e_sem.at[0], e_sem.at[1], {"outer": (o + d) % nout})

    def e_second(d):
        return remote(earlyz.at[0], earlyz.at[nz - d], ez_sem.at[0], ez_sem.at[1], {"row": (z + d) % nz})

    for h in range(len(fine)):
        for s in range(nz - 2, nz):
            for zz in (z - s, z + s):
                @pl.when((zz >= 0) & (zz < nz) & (zz != mate))
                def _():
                    take(zz, h)

        take_mate(h)
        if h == last:
            settle(early.at[pl.ds(1, nout - 1)], e_sem.at[1])
            earlyz[0] = jnp.sum(early[...], axis=0)
            for d in range(1, nz):
                e_second(d).start()
        finish(h, h == last)
        if fine[h][0] + fine[h][1] == wide:
            for d in range(1, nout):
                e_first(d).start()
            for d in range(1, ncol):
                pl.semaphore_signal(ready, inc=1, device_id={"col": (x + d) % ncol}, device_id_type=MESH)

    group = nout * nz
    rest = width - wide

    def mirror(k):
        return ((nout - k // nz) % nout) * nz + (nz - k % nz) % nz

    def peer(k, c):
        return {"outer": (o + k // nz) % nout, "row": (z + k % nz) % nz, "col": (x + c) % ncol}

    def send_late(k):
        remote(late.at[0], late.at[mirror(k)], l_sem.at[0], l_sem.at[1], peer(k, 0)).start()

    late[0, :, pl.ds(rest, 128)] = jnp.sum(rowp[...], axis=0, keepdims=True) * ((1.0 - decay) / F) + old_share
    each(1, group, send_late)
    pl.semaphore_wait(ready, ncol - 1)
    for d in range(1, ncol):
        def send_other(k):
            slot = (ncol - d - 1) * group + mirror(k)
            remote(late.at[0, :, pl.ds(rest, 128)], others.at[slot], o_sem.at[0], o_sem.at[1], peer(k, d)).start()

        each(0, group, send_other)
    rowbuf[0] = jnp.sum(jnp.transpose(rowp[...]), axis=0, keepdims=True)

    def r_first(d):
        return remote(rowbuf.at[0], rowbuf.at[ncol - d], r_sem.at[0], r_sem.at[1], {"col": (x + d) % ncol})

    for d in range(1, ncol):
        r_first(d).start()
    settle(rowbuf.at[pl.ds(1, ncol - 1)], r_sem.at[1])
    row_sq = jnp.sum(rowbuf[...], axis=0)
    new_row = decay * old + (1.0 - decay) * row_sq / F
    nr_ref[...] = new_row
    byrow_ref[...] = jnp.transpose(jnp.broadcast_to(lax.rsqrt(new_row), (128, rows)))
    settle(earlyz.at[pl.ds(1, nz - 1)], ez_sem.at[1])
    cm = cm_ref[...].reshape(1, width)
    new_early = decay * cm[:, :wide] + (1.0 - decay) * jnp.sum(earlyz[...], axis=0) / D
    nc_ref[:, :wide] = new_early
    settle(late.at[pl.ds(1, group - 1)], l_sem.at[1])
    arrived = jnp.sum(late[...], axis=0)
    new_late = decay * cm[:, wide:] + (1.0 - decay) * arrived[:, :rest] / D
    nc_ref[:, wide:] = new_late
    settle(others, o_sem.at[1])
    total = jnp.sum(arrived[:, rest:] + jnp.sum(others[...], axis=0), axis=1, keepdims=True)
    factor = D / total
    bycol_ref[:, :wide] = lax.rsqrt(new_early * factor)
    bycol_ref[:, wide:] = lax.rsqrt(new_late * factor)

    for k in range(nz):
        if k < nz - 1:
            @pl.when(z == k)
            def _():
                settle(slots(0, 0, k + 1, full), zp_send)

        if k > 0:
            @pl.when(z == k)
            def _():
                settle(slots(0, 0, nz - k, full), zm_send)

    settle(slots(0, 0, nz - 1, full), y_send.at[0])
    settle(slots(0, 0, 1, by_y), y_send.at[1])
    settle(slots(0, 0, 2 * nz, full), p_send)
    settle(slots(0, 0, 1, (by_y[1], width - by_y[1])), x_send)
    settle(av.at[pl.ds(0, nout - 1)], a1_send)
    settle(av.at[pl.ds(0, (ncol - 1) * nout)], a2_send)
    settle(early.at[pl.ds(1, nout - 1)], e_sem.at[0])
    settle(earlyz.at[pl.ds(1, nz - 1)], ez_sem.at[0])
    settle(late.at[pl.ds(1, group - 1)], l_sem.at[0])
    settle(others, o_sem.at[0])
    settle(rowbuf.at[pl.ds(1, ncol - 1)], r_sem.at[0])


def update_kernel(step, grad_ref, byrow_ref, bycol_ref, nr_ref, nc_ref, out_hbm, row_hbm, col_hbm, out, row, col, sem):
    parts = out.shape[0] // step
    row[...] = nr_ref[...].reshape(row.shape)
    col[...] = nc_ref[...].reshape(col.shape)
    copies = [
        pltpu.make_async_copy(row, row_hbm, sem.at[parts]),
        pltpu.make_async_copy(col, col_hbm, sem.at[parts + 1]),
    ]
    for c in copies:
        c.start()
    for k in range(parts):
        here = pl.ds(k * step, step)
        out[here, :] = (grad_ref[here, :] * byrow_ref[here, :1] * bycol_ref[...]).astype(out.dtype)
        copies.append(pltpu.make_async_copy(out.at[here], out_hbm.at[here], sem.at[k]))
        copies[-1].start()
    for c in copies:
        c.wait()


def body(nout, nz, ncol, activations, out_grads, row_moment, col_moment):
    rows, width = row_moment.shape[0], col_moment.shape[0]
    ta, tg = activations.shape[0], out_grads.shape[0]
    tokens = ta * ncol * nout
    decay = 1.0 - STEP ** (-0.8)
    f32, bf16 = jnp.float32, jnp.bfloat16
    vmem = pl.BlockSpec(memory_space=pltpu.VMEM)
    hbm = pl.BlockSpec(memory_space=pl.ANY)
    dma = pltpu.SemaphoreType.DMA
    fine, chain, _, _ = cuts(width)
    wide = fine[1][0] + fine[1][1]
    grad, new_row, by_row, new_col, by_col = pl.pallas_call(
        functools.partial(kernel, nout, nz, ncol, 1.0 / tokens**0.5, decay),
        out_shape=(
            pltpu.VMEM((rows, width), f32),
            pltpu.VMEM((1, rows), f32),
            pltpu.VMEM((rows, 128), f32),
            pltpu.VMEM((1, width), f32),
            pltpu.VMEM((1, width), f32),
        ),
        in_specs=[hbm] * 4,
        out_specs=(vmem,) * 5,
        scratch_shapes=[
            pltpu.VMEM((tokens, width), bf16),
            pltpu.VMEM((nout * ncol, rows, ta), bf16),
            pltpu.VMEM(activations.shape, bf16),
            pltpu.VMEM((nout, rows, ta), bf16),
            pltpu.VMEM((rows,), f32),
            pltpu.VMEM((width,), f32),
            pltpu.VMEM((rows, 128), f32),
            pltpu.VMEM((nout, 1, wide), f32),
            pltpu.VMEM((nz, 1, wide), f32),
            pltpu.VMEM((nout * nz, 1, width - wide + 128), f32),
            pltpu.VMEM(((ncol - 1) * nout * nz, 1, 128), f32),
            pltpu.VMEM((ncol, 1, rows), f32),
            dma((nz, len(chain))),
            dma((nz, len(fine) + 1)),
            dma((len(chain),)),
            dma((len(fine),)),
            dma((nout,)),
            dma(()),
            dma(()),
            dma(()),
            dma(()),
            dma((2,)),
            dma(()),
            dma(()),
            dma(()),
            dma((5,)),
            dma((2,)), dma((2,)), dma((2,)), dma((2,)), dma((2,)),
            pltpu.SemaphoreType.REGULAR,
        ],
        compiler_params=pltpu.CompilerParams(
            collective_id=0, has_side_effects=True, vmem_limit_bytes=44 * 1024 * 1024
        ),
    )(
        activations,
        out_grads,
        pltpu.with_memory_space_constraint(row_moment, pltpu.HBM),
        pltpu.with_memory_space_constraint(col_moment, pltpu.HBM),
    )
    parts = next(n for n in (9, 6, 4, 3, 2, 1) if n == 1 or rows % (n * 16) == 0)
    return pl.pallas_call(
        functools.partial(update_kernel, rows // parts),
        out_shape=(
            jax.ShapeDtypeStruct((rows, width), bf16),
            jax.ShapeDtypeStruct((rows,), f32),
            jax.ShapeDtypeStruct((width,), f32),
        ),
        in_specs=[vmem] * 5,
        out_specs=(hbm,) * 3,
        scratch_shapes=[
            pltpu.VMEM((rows, width), bf16),
            pltpu.VMEM((rows,), f32),
            pltpu.VMEM((width,), f32),
            dma((parts + 2,)),
        ],
        compiler_params=pltpu.CompilerParams(vmem_limit_bytes=24 * 1024 * 1024),
    )(grad, by_row, by_col, new_row, new_col)


def solution(mesh):
    nout, nz, ncol = mesh.shape["outer"], mesh.shape["row"], mesh.shape["col"]
    return jax.shard_map(
        functools.partial(body, nout, nz, ncol),
        mesh=mesh,
        in_specs=(
            P(("outer", "col"), "row"),
            P(("outer", "row"), "col"),
            P(("row", "outer")),
            P("col"),
        ),
        out_specs=(P(("row", "outer"), "col"), P(("row", "outer")), P("col")),
        check_vma=False,
    )
```

time: 111 us -> 105 us (0.946)
  Pallas kernels: 109 us -> 104 us
  local copies, waits for them, and re-layouts: 1.4 us -> 0 us
    pallas_call x1, Pallas kernels: 106 us -> 101 us  [body(): pl.pallas_call(functools.partial(kernel, nout, nz, ncol, 1.0 / tokens **...]
    unnamed x4 -> x0, local copies, waits for them, and re-layouts: 1.4 us -> none
where the time goes in v1:
time: 105 us; the launch traced here: 104 us
  Pallas kernels  104 us (99%)
    pallas_call x1, Pallas kernels, body(): pl.pallas_call(functools.partial(kernel, nout, nz, ncol, 1.0 / tokens **...  101 us
    pallas_call x1, Pallas kernels, body(): pl.pallas_call(functools.partial(update_kernel, rows // parts), out_shape...  2.47 us

profile of v1, /device:TPU:0, one launch (start us, length us, event | category | flops | bytes accessed | tf_op | source)
XLA Modules:
  0.0 104.4 jit_solution(8966072886105427487)
XLA Ops:
  0.6 101.3 %shard_map.67 = (f32[576,4096]{1,0:T(8,128)S(1)}, f32[1,576]{1,0:T(1,128)S(1)}, f32[576,128]{1,0:T(8,128)S(1)}, f32[1,4096]{1,0:T(1,128)S(1)}, f32[1,4096]{1,0:T(1,128)S(1)}) custom-call(bf16[256,2304]{1,0:T(8,128)(2,1)} %raw_ref.1, bf16[128,4096]{1,0:T(8,128)(2,1)} %g_ref.1, f32[576]{0:T(1024)} %rm_hbm.1, f32[4096]{0:T(1024)} %cm_hbm.1), custom_call_target="tpu_custom_call" | custom-call | tf_op jit(solution)/shard_map/pallas_call | solution.py:443
  101.9 2.5 %shard_map.68 = (bf16[576,4096]{1,0:T(8,128)(2,1)}, f32[576]{0:T(1024)}, f32[4096]{0:T(1024)}) custom-call(f32[576,4096]{1,0:T(8,128)S(1)} %get-tuple-element.8.grad_ref, f32[576,128]{1,0:T(8,128)S(1)} %get-tuple-element.9.byrow_ref, f32[1,4096]{1,0:T(1,128)S(1)} %get-tuple-element.10.bycol_ref, f32[1,576]{1,0:T(1,128)S(1)} %get-tuple-element.11.nr_ref, ...), custom_call_target="tpu_custom_call" | custom-call | tf_op jit(solution)/shard_map/pallas_call | solution.py:494

commit v2 on v1

--- a/solution.py
+++ b/solution.py
@@ -15,9 +15,10 @@
 
 def cuts(width):
     unit = width // 128
-    share, *edges = [round(unit * e / 32) * 128 for e in (7, 16, 24, 28, 32)]
+    edges = [round(unit * e / 32) * 128 for e in (8, 16, 24, 28, 32)]
+    share = min(round(unit * 7 / 32) * 128, edges[0] - 128)
     fine = [(a, b - a) for a, b in zip([0] + edges[:-1], edges)]
-    chain = [[0], [1], [2, 3]]
+    chain = [[0, 1], [2], [3, 4]]
     by_y = (0, share)
     by_z = [(share, edges[0] - share)] + fine[1:]
     return fine, chain, by_y, by_z
@@ -36,7 +37,7 @@
     raw_ref, g_ref, rm_hbm, cm_hbm,
     acc, nr_ref, byrow_ref, nc_ref, bycol_ref,
     gs, av, raw, a_ref, rm_ref, cm_ref, rowp, early, earlyz, late, others, rowbuf,
-    gz_recv, gy_recv, op_recv, od_recv, a1_recv, a2_recv,
+    gz_recv, gy_recv, far_recv, mate_recv, op_recv, od_recv, a1_recv, a2_recv,
     zp_send, zm_send, x_send, y_send, p_send, a1_send, a2_send, loc_sem,
     e_sem, ez_sem, l_sem, o_sem, r_sem, ready,
 ):
@@ -53,6 +54,7 @@
     op = y * 2 + (1 - core)
     od = (1 - y) * 2 + (1 - core)
     mate = z + 1 - 2 * (z % 2)
+    end = jnp.where(z < nz // 2, nz - 1, 0)
     up = {"row": jnp.minimum(z + 1, nz - 1)}
     down = {"row": jnp.maximum(z - 1, 0)}
 
@@ -64,10 +66,10 @@
     def settle(ref, sem):
         pltpu.make_async_copy(ref, ref, sem).wait()
 
-    load_a = pltpu.make_async_copy(raw_ref, raw, loc_sem.at[2])
+    load_a = pltpu.make_async_copy(raw_ref, raw, loc_sem.at[1])
     load_a.start()
-    load_rm = pltpu.make_async_copy(rm_hbm, rm_ref, loc_sem.at[3])
-    load_cm = pltpu.make_async_copy(cm_hbm, cm_ref, loc_sem.at[4])
+    load_rm = pltpu.make_async_copy(rm_hbm, rm_ref, loc_sem.at[2])
+    load_cm = pltpu.make_async_copy(cm_hbm, cm_ref, loc_sem.at[3])
     load_rm.start()
     load_cm.start()
     barrier = pltpu.get_barrier_semaphore()
@@ -100,19 +102,22 @@
 
     full = (0, width)
 
+    def from_z(zz, c, at):
+        return gz_recv.at[(zz - at - 1 + 2 * nz) % nz, c]
+
     def to_up(src, zz, c):
-        return remote(src, place(o, zz, merged(c)), zp_send, gz_recv.at[zz, c], up)
+        return remote(src, place(o, zz, merged(c)), zp_send, from_z(zz, c, z + 1), up)
 
     def to_down(src, zz, c):
-        return remote(src, place(o, zz, merged(c)), zm_send, gz_recv.at[zz, c], down)
-
-    def to_y(src, zz, cols, j, sem):
-        return remote(src, place(o, zz, cols), sem, gy_recv.at[zz, j], {"outer": oy})
+        return remote(src, place(o, zz, merged(c)), zm_send, from_z(zz, c, z - 1), down)
+
+    def to_y(src, zz, cols, sem, got):
+        return remote(src, place(o, zz, cols), sem, got, {"outer": oy})
 
     def near(src, zz, c):
         return remote(src, place(o, zz, merged(c)), p_send, op_recv.at[c], {"outer": op})
 
-    def far(zz, cols, h):
+    def over(zz, cols, h):
         here = place(oy, zz, cols)
         return remote(here, here, p_send, od_recv.at[h], {"outer": op})
 
@@ -128,12 +133,12 @@
             to_down(own, z, c).start()
 
         if c == 0:
-            to_y(g_ref, z, full, 0, y_send.at[0]).start()
+            to_y(g_ref, z, full, y_send.at[0], gy_recv.at[z]).start()
         near(own, z, c).start()
 
     def a_first(d):
         target = (o + d) % nout
-        return remote(a_ref.at[target], av.at[o * ncol + x], a1_send, a1_recv.at[o], {"outer": target})
+        return remote(a_ref.at[target], av.at[o * ncol + x], a1_send, a1_recv.at[d - 1], {"outer": target})
 
     def a_second(oo, d, own=False):
         k = oo * ncol + x
@@ -149,53 +154,60 @@
 
     def pass_on(oo):
         k = oo * ncol + x
-        remote(av.at[k], av.at[k], a1_send, a1_recv.at[oo], {"outer": oy}).wait_recv()
+        remote(av.at[k], av.at[k], a1_send, a1_recv.at[(o - oo + nout) % nout - 1], {"outer": oy}).wait_recv()
         for d in range(1, ncol):
             a_second(oo, d).start()
 
-    def landed(zz, cols, j):
+    def landed(zz, cols, sem):
         here = place(oy, zz, cols)
-        remote(here, here, y_send.at[0], gy_recv.at[zz, j], {"outer": oy}).wait_recv()
-
-    def take(zz, h):
-        landed(zz, fine[h], h)
-        far(zz, fine[h], h).start()
-
-    def take_mate(h):
+        remote(here, here, y_send.at[0], sem, {"outer": oy}).wait_recv()
+
+    def take_whole(zz):
+        landed(zz, full, gy_recv.at[zz])
+        for h in range(len(fine)):
+            over(zz, fine[h], h).start()
+
+    def take(h):
+        landed(end, fine[h], far_recv.at[h])
+        over(end, fine[h], h).start()
         if h == 0:
-            landed(mate, by_y, 0)
-            far(mate, by_y, 0).start()
-        landed(mate, by_z[h], h + 1)
-        far(mate, by_z[h], h).start()
+            landed(mate, by_y, mate_recv.at[0])
+            over(mate, by_y, 0).start()
+        landed(mate, by_z[h], mate_recv.at[h + 1])
+        over(mate, by_z[h], h).start()
 
     def relay(zz, c, onward):
         here = place(o, zz, merged(c))
-        remote(here, here, zp_send, gz_recv.at[zz, c], up).wait_recv()
+        remote(here, here, zp_send, from_z(zz, c, z), up).wait_recv()
         onward(here)
 
-        @pl.when(zz != mate)
+        @pl.when((zz != mate) & (zz != end))
+        def _():
+            to_y(here, zz, merged(c), y_send.at[0], gy_recv.at[zz]).start()
+
+        @pl.when(zz == end)
         def _():
             for j in chain[c]:
-                to_y(place(o, zz, fine[j]), zz, fine[j], j, y_send.at[0]).start()
+                to_y(place(o, zz, fine[j]), zz, fine[j], y_send.at[0], far_recv.at[j]).start()
 
         if c == 0:
             @pl.when(zz == mate)
             def _():
-                to_y(place(o, zz, by_y), zz, by_y, 0, y_send.at[1]).start()
+                to_y(place(o, zz, by_y), zz, by_y, y_send.at[1], mate_recv.at[0]).start()
 
         near(here, zz, c).start()
 
-    def extra(act):
+    def extra():
         for h in range(len(fine)):
             here = place(oy, z, by_z[h])
 
             @pl.when(mate > z)
             def _():
-                act(remote(here, here, x_send, gy_recv.at[z, h + 1], up))
+                remote(here, here, x_send, mate_recv.at[h + 1], up).start()
 
             @pl.when(mate < z)
             def _():
-                act(remote(here, here, x_send, gy_recv.at[z, h + 1], down))
+                remote(here, here, x_send, mate_recv.at[h + 1], down).start()
 
     def dots(oo, cols):
         total = None
@@ -228,6 +240,12 @@
 
         tiles(merged(c), one)
 
+    def whole_from(d):
+        for zz in (z - d, z + d):
+            @pl.when((zz >= 0) & (zz < nz) & (zz != mate) & (zz != end))
+            def _():
+                take_whole(zz)
+
     for s in range(1, nz):
         if s == nz - 1:
             local_g.wait()
@@ -260,23 +278,20 @@
                 local_a.start()
             if s == nz - 1:
                 first_half(c)
+                if c == len(chain) - 2:
+                    for d in (nz - 2, nz - 1):
+                        whole_from(d)
 
         if s == 1:
-            landed(z, full, 0)
-            for h in range(len(fine)):
-                far(z, fine[h], h).start()
+            take_whole(z)
             pass_on(op)
         if s == min(2, nz - 1):
             for c in range(2):
                 pass_on((1 - y) * 2 + c)
         if s == max(nz - 2, 1):
-            extra(lambda c: c.start())
+            extra()
         if 1 < s < nz - 1:
-            for zz in (z - (s - 1), z + (s - 1)):
-                @pl.when((zz >= 0) & (zz < nz) & (zz != mate))
-                def _():
-                    for h in range(len(fine)):
-                        take(zz, h)
+            whole_from(s - 1)
 
     rowp[...] = jnp.zeros_like(rowp)
     load_rm.wait()
@@ -320,18 +335,7 @@
         return remote(earlyz.at[0], earlyz.at[nz - d], ez_sem.at[0], ez_sem.at[1], {"row": (z + d) % nz})
 
     for h in range(len(fine)):
-        for s in range(nz - 2, nz):
-            for zz in (z - s, z + s):
-                @pl.when((zz >= 0) & (zz < nz) & (zz != mate))
-                def _():
-                    take(zz, h)
-
-        take_mate(h)
-        if h == last:
-            settle(early.at[pl.ds(1, nout - 1)], e_sem.at[1])
-            earlyz[0] = jnp.sum(early[...], axis=0)
-            for d in range(1, nz):
-                e_second(d).start()
+        take(h)
         finish(h, h == last)
         if fine[h][0] + fine[h][1] == wide:
             for d in range(1, nout):
@@ -352,7 +356,6 @@
         remote(late.at[0], late.at[mirror(k)], l_sem.at[0], l_sem.at[1], peer(k, 0)).start()
 
     late[0, :, pl.ds(rest, 128)] = jnp.sum(rowp[...], axis=0, keepdims=True) * ((1.0 - decay) / F) + old_share
-    each(1, group, send_late)
     pl.semaphore_wait(ready, ncol - 1)
     for d in range(1, ncol):
         def send_other(k):
@@ -360,6 +363,11 @@
             remote(late.at[0, :, pl.ds(rest, 128)], others.at[slot], o_sem.at[0], o_sem.at[1], peer(k, d)).start()
 
         each(0, group, send_other)
+    each(1, group, send_late)
+    settle(early.at[pl.ds(1, nout - 1)], e_sem.at[1])
+    earlyz[0] = jnp.sum(early[...], axis=0)
+    for d in range(1, nz):
+        e_second(d).start()
     rowbuf[0] = jnp.sum(jnp.transpose(rowp[...]), axis=0, keepdims=True)
 
     def r_first(d):
@@ -422,7 +430,7 @@
         c.start()
     for k in range(parts):
         here = pl.ds(k * step, step)
-        out[here, :] = (grad_ref[here, :] * byrow_ref[here, :1] * bycol_ref[...]).astype(out.dtype)
+        out[here, :] = (grad_ref[here, :] * jnp.tile(byrow_ref[here, :], (1, out.shape[1] // 128)) * bycol_ref[...]).astype(out.dtype)
         copies.append(pltpu.make_async_copy(out.at[here], out_hbm.at[here], sem.at[k]))
         copies[-1].start()
     for c in copies:
@@ -439,7 +447,7 @@
     hbm = pl.BlockSpec(memory_space=pl.ANY)
     dma = pltpu.SemaphoreType.DMA
     fine, chain, _, _ = cuts(width)
-    wide = fine[1][0] + fine[1][1]
+    wide = fine[2][0] + fine[2][1]
     grad, new_row, by_row, new_col, by_col = pl.pallas_call(
         functools.partial(kernel, nout, nz, ncol, 1.0 / tokens**0.5, decay),
         out_shape=(
@@ -464,11 +472,13 @@
             pltpu.VMEM((nout * nz, 1, width - wide + 128), f32),
             pltpu.VMEM(((ncol - 1) * nout * nz, 1, 128), f32),
             pltpu.VMEM((ncol, 1, rows), f32),
-            dma((nz, len(chain))),
-            dma((nz, len(fine) + 1)),
+            dma((nz - 1, len(chain))),
+            dma((nz,)),
+            dma((len(fine),)),
+            dma((len(fine) + 1,)),
             dma((len(chain),)),
             dma((len(fine),)),
-            dma((nout,)),
+            dma((nout - 1,)),
             dma(()),
             dma(()),
             dma(()),
@@ -477,7 +487,7 @@
             dma(()),
             dma(()),
             dma(()),
-            dma((5,)),
+            dma((4,)),
             dma((2,)), dma((2,)), dma((2,)), dma((2,)), dma((2,)),
             pltpu.SemaphoreType.REGULAR,
         ],

time: 105 us -> 103 us (0.981)
  Pallas kernels: 104 us -> 102 us
    pallas_call x1, Pallas kernels: 101 us -> 99.9 us  [body(): pl.pallas_call(functools.partial(kernel, nout, nz, ncol, 1.0 / tokens **...]
where the time goes in v2:
time: 103 us
  Pallas kernels  102 us (99%)
    pallas_call x1, Pallas kernels, body(): pl.pallas_call(functools.partial(kernel, nout, nz, ncol, 1.0 / tokens **...  99.9 us
    pallas_call x1, Pallas kernels, body(): pl.pallas_call(functools.partial(update_kernel, rows // parts), out_shape...  2.37 us

profile of v2, /device:TPU:0, one launch (start us, length us, event | category | flops | bytes accessed | tf_op | source)
XLA Modules:
  0.0 102.9 jit_solution(14835327606932131605)
XLA Ops:
  0.6 99.9 %shard_map.67 = (f32[576,4096]{1,0:T(8,128)S(1)}, f32[1,576]{1,0:T(1,128)S(1)}, f32[576,128]{1,0:T(8,128)S(1)}, f32[1,4096]{1,0:T(1,128)S(1)}, f32[1,4096]{1,0:T(1,128)S(1)}) custom-call(bf16[256,2304]{1,0:T(8,128)(2,1)} %raw_ref.1, bf16[128,4096]{1,0:T(8,128)(2,1)} %g_ref.1, f32[576]{0:T(1024)} %rm_hbm.1, f32[4096]{0:T(1024)} %cm_hbm.1), custom_call_target="tpu_custom_call" | custom-call | tf_op jit(solution)/shard_map/pallas_call | solution.py:451
  100.6 2.4 %shard_map.68 = (bf16[576,4096]{1,0:T(8,128)(2,1)}, f32[576]{0:T(1024)}, f32[4096]{0:T(1024)}) custom-call(f32[576,4096]{1,0:T(8,128)S(1)} %get-tuple-element.8.grad_ref, f32[576,128]{1,0:T(8,128)S(1)} %get-tuple-element.9.byrow_ref, f32[1,4096]{1,0:T(1,128)S(1)} %get-tuple-element.10.bycol_ref, f32[1,576]{1,0:T(1,128)S(1)} %get-tuple-element.11.nr_ref, ...), custom_call_target="tpu_custom_call" | custom-call | tf_op jit(solution)/shard_map/pallas_call | solution.py:504

commit v3 on v2

--- a/solution.py
+++ b/solution.py
@@ -38,7 +38,7 @@
     acc, nr_ref, byrow_ref, nc_ref, bycol_ref,
     gs, av, raw, a_ref, rm_ref, cm_ref, rowp, early, earlyz, late, others, rowbuf,
     gz_recv, gy_recv, far_recv, mate_recv, op_recv, od_recv, a1_recv, a2_recv,
-    zp_send, zm_send, x_send, y_send, p_send, a1_send, a2_send, loc_sem,
+    g_send, p_send, a_send, loc_sem,
     e_sem, ez_sem, l_sem, o_sem, r_sem, ready,
 ):
     tg, width = g_ref.shape
@@ -106,10 +106,10 @@
         return gz_recv.at[(zz - at - 1 + 2 * nz) % nz, c]
 
     def to_up(src, zz, c):
-        return remote(src, place(o, zz, merged(c)), zp_send, from_z(zz, c, z + 1), up)
+        return remote(src, place(o, zz, merged(c)), g_send, from_z(zz, c, z + 1), up)
 
     def to_down(src, zz, c):
-        return remote(src, place(o, zz, merged(c)), zm_send, from_z(zz, c, z - 1), down)
+        return remote(src, place(o, zz, merged(c)), g_send, from_z(zz, c, z - 1), down)
 
     def to_y(src, zz, cols, sem, got):
         return remote(src, place(o, zz, cols), sem, got, {"outer": oy})
@@ -133,16 +133,16 @@
             to_down(own, z, c).start()
 
         if c == 0:
-            to_y(g_ref, z, full, y_send.at[0], gy_recv.at[z]).start()
+            to_y(g_ref, z, full, g_send, gy_recv.at[z]).start()
         near(own, z, c).start()
 
     def a_first(d):
         target = (o + d) % nout
-        return remote(a_ref.at[target], av.at[o * ncol + x], a1_send, a1_recv.at[d - 1], {"outer": target})
+        return remote(a_ref.at[target], av.at[o * ncol + x], a_send, a1_recv.at[d - 1], {"outer": target})
 
     def a_second(oo, d, own=False):
         k = oo * ncol + x
-        return remote(a_ref.at[o] if own else av.at[k], av.at[k], a2_send, a2_recv, {"col": (x + d) % ncol})
+        return remote(a_ref.at[o] if own else av.at[k], av.at[k], a_send, a2_recv, {"col": (x + d) % ncol})
 
     local_g = pltpu.make_async_copy(g_ref, slots(o, z, 1, full), loc_sem.at[0])
     local_a = pltpu.make_async_copy(a_ref.at[o], av.at[o * ncol + x], loc_sem.at[1])
@@ -154,13 +154,13 @@
 
     def pass_on(oo):
         k = oo * ncol + x
-        remote(av.at[k], av.at[k], a1_send, a1_recv.at[(o - oo + nout) % nout - 1], {"outer": oy}).wait_recv()
+        remote(av.at[k], av.at[k], a_send, a1_recv.at[(o - oo + nout) % nout - 1], {"outer": oy}).wait_recv()
         for d in range(1, ncol):
             a_second(oo, d).start()
 
     def landed(zz, cols, sem):
         here = place(oy, zz, cols)
-        remote(here, here, y_send.at[0], sem, {"outer": oy}).wait_recv()
+        remote(here, here, g_send, sem, {"outer": oy}).wait_recv()
 
     def take_whole(zz):
         landed(zz, full, gy_recv.at[zz])
@@ -170,30 +170,27 @@
     def take(h):
         landed(end, fine[h], far_recv.at[h])
         over(end, fine[h], h).start()
-        if h == 0:
-            landed(mate, by_y, mate_recv.at[0])
-            over(mate, by_y, 0).start()
-        landed(mate, by_z[h], mate_recv.at[h + 1])
-        over(mate, by_z[h], h).start()
+        landed(mate, fine[h], mate_recv.at[h])
+        over(mate, fine[h], h).start()
 
     def relay(zz, c, onward):
         here = place(o, zz, merged(c))
-        remote(here, here, zp_send, from_z(zz, c, z), up).wait_recv()
+        remote(here, here, g_send, from_z(zz, c, z), up).wait_recv()
         onward(here)
 
         @pl.when((zz != mate) & (zz != end))
         def _():
-            to_y(here, zz, merged(c), y_send.at[0], gy_recv.at[zz]).start()
+            to_y(here, zz, merged(c), g_send, gy_recv.at[zz]).start()
 
         @pl.when(zz == end)
         def _():
             for j in chain[c]:
-                to_y(place(o, zz, fine[j]), zz, fine[j], y_send.at[0], far_recv.at[j]).start()
+                to_y(place(o, zz, fine[j]), zz, fine[j], g_send, far_recv.at[j]).start()
 
         if c == 0:
             @pl.when(zz == mate)
             def _():
-                to_y(place(o, zz, by_y), zz, by_y, y_send.at[1], mate_recv.at[0]).start()
+                to_y(place(o, zz, by_y), zz, by_y, g_send, mate_recv.at[0]).start()
 
         near(here, zz, c).start()
 
@@ -203,11 +200,11 @@
 
             @pl.when(mate > z)
             def _():
-                remote(here, here, x_send, mate_recv.at[h + 1], up).start()
+                remote(here, here, g_send, mate_recv.at[h], up).start()
 
             @pl.when(mate < z)
             def _():
-                remote(here, here, x_send, mate_recv.at[h + 1], down).start()
+                remote(here, here, g_send, mate_recv.at[h], down).start()
 
     def dots(oo, cols):
         total = None
@@ -334,8 +331,20 @@
     def e_second(d):
         return remote(earlyz.at[0], earlyz.at[nz - d], ez_sem.at[0], ez_sem.at[1], {"row": (z + d) % nz})
 
+    @pl.when(core == 1)
+    def _():
+        take(0)
+
     for h in range(len(fine)):
-        take(h)
+        @pl.when(core == 0)
+        def _():
+            take(h)
+
+        if h < last:
+            @pl.when(core == 1)
+            def _():
+                take(h + 1)
+
         finish(h, h == last)
         if fine[h][0] + fine[h][1] == wide:
             for d in range(1, nout):
@@ -394,23 +403,18 @@
     bycol_ref[:, :wide] = lax.rsqrt(new_early * factor)
     bycol_ref[:, wide:] = lax.rsqrt(new_late * factor)
 
-    for k in range(nz):
-        if k < nz - 1:
-            @pl.when(z == k)
-            def _():
-                settle(slots(0, 0, k + 1, full), zp_send)
-
-        if k > 0:
-            @pl.when(z == k)
-            def _():
-                settle(slots(0, 0, nz - k, full), zm_send)
-
-    settle(slots(0, 0, nz - 1, full), y_send.at[0])
-    settle(slots(0, 0, 1, by_y), y_send.at[1])
+    at_end = (z == 0) | (z == nz - 1)
+
+    @pl.when(at_end)
+    def _():
+        settle(slots(0, 0, nz + 1, full), g_send)
+
+    @pl.when(jnp.logical_not(at_end))
+    def _():
+        settle(slots(0, 0, 2 * nz + 1, full), g_send)
+
     settle(slots(0, 0, 2 * nz, full), p_send)
-    settle(slots(0, 0, 1, (by_y[1], width - by_y[1])), x_send)
-    settle(av.at[pl.ds(0, nout - 1)], a1_send)
-    settle(av.at[pl.ds(0, (ncol - 1) * nout)], a2_send)
+    settle(av.at[pl.ds(0, ncol * nout - 1)], a_send)
     settle(early.at[pl.ds(1, nout - 1)], e_sem.at[0])
     settle(earlyz.at[pl.ds(1, nz - 1)], ez_sem.at[0])
     settle(late.at[pl.ds(1, group - 1)], l_sem.at[0])
@@ -475,15 +479,11 @@
             dma((nz - 1, len(chain))),
             dma((nz,)),
             dma((len(fine),)),
-            dma((len(fine) + 1,)),
+            dma((len(fine),)),
             dma((len(chain),)),
             dma((len(fine),)),
             dma((nout - 1,)),
             dma(()),
-            dma(()),
-            dma(()),
-            dma(()),
-            dma((2,)),
             dma(()),
             dma(()),
             dma(()),

time: 103 us -> 102 us (level)
    pallas_call x1, Pallas kernels: 99.9 us -> 98.9 us  [body(): pl.pallas_call(functools.partial(kernel, nout, nz, ncol, 1.0 / tokens **...]
where the time goes in v3:
time: 102 us
  Pallas kernels  101 us (99%)
    pallas_call x1, Pallas kernels, body(): pl.pallas_call(functools.partial(kernel, nout, nz, ncol, 1.0 / tokens **...  98.9 us
    pallas_call x1, Pallas kernels, body(): pl.pallas_call(functools.partial(update_kernel, rows // parts), out_shape...  2.37 us

profile of v3, /device:TPU:0, one launch (start us, length us, event | category | flops | bytes accessed | tf_op | source)
XLA Modules:
  0.0 101.9 jit_solution(8976792183236394575)
XLA Ops:
  0.6 98.9 %shard_map.67 = (f32[576,4096]{1,0:T(8,128)S(1)}, f32[1,576]{1,0:T(1,128)S(1)}, f32[576,128]{1,0:T(8,128)S(1)}, f32[1,4096]{1,0:T(1,128)S(1)}, f32[1,4096]{1,0:T(1,128)S(1)}) custom-call(bf16[256,2304]{1,0:T(8,128)(2,1)} %raw_ref.1, bf16[128,4096]{1,0:T(8,128)(2,1)} %g_ref.1, f32[576]{0:T(1024)} %rm_hbm.1, f32[4096]{0:T(1024)} %cm_hbm.1), custom_call_target="tpu_custom_call" | custom-call | tf_op jit(solution)/shard_map/pallas_call | solution.py:455
  99.5 2.4 %shard_map.68 = (bf16[576,4096]{1,0:T(8,128)(2,1)}, f32[576]{0:T(1024)}, f32[4096]{0:T(1024)}) custom-call(f32[576,4096]{1,0:T(8,128)S(1)} %get-tuple-element.8.grad_ref, f32[576,128]{1,0:T(8,128)S(1)} %get-tuple-element.9.byrow_ref, f32[1,4096]{1,0:T(1,128)S(1)} %get-tuple-element.10.bycol_ref, f32[1,576]{1,0:T(1,128)S(1)} %get-tuple-element.11.nr_ref, ...), custom_call_target="tpu_custom_call" | custom-call | tf_op jit(solution)/shard_map/pallas_call | solution.py:504

commit v4 on v3

--- a/solution.py
+++ b/solution.py
@@ -15,8 +15,7 @@
 
 def cuts(width):
     unit = width // 128
-    edges = [round(unit * e / 32) * 128 for e in (8, 16, 24, 28, 32)]
-    share = min(round(unit * 7 / 32) * 128, edges[0] - 128)
+    share, *edges = [unit * e // 32 * 128 for e in (7, 8, 16, 24, 30, 32)]
     fine = [(a, b - a) for a, b in zip([0] + edges[:-1], edges)]
     chain = [[0, 1], [2], [3, 4]]
     by_y = (0, share)
@@ -68,13 +67,11 @@
 
     load_a = pltpu.make_async_copy(raw_ref, raw, loc_sem.at[1])
     load_a.start()
-    load_rm = pltpu.make_async_copy(rm_hbm, rm_ref, loc_sem.at[2])
-    load_cm = pltpu.make_async_copy(cm_hbm, cm_ref, loc_sem.at[3])
-    load_rm.start()
-    load_cm.start()
+    load_rm = pltpu.make_async_copy(rm_hbm, rm_ref, loc_sem.at[0])
+    load_cm = pltpu.make_async_copy(cm_hbm, cm_ref, loc_sem.at[1])
     barrier = pltpu.get_barrier_semaphore()
-    for d in range(1, nout):
-        pl.semaphore_signal(barrier, inc=1, device_id={"outer": (o + d) % nout}, device_id_type=MESH)
+    for who in (oy, op):
+        pl.semaphore_signal(barrier, inc=1, device_id={"outer": who}, device_id_type=MESH)
 
     @pl.when(z > 0)
     def _():
@@ -87,7 +84,7 @@
     for d in range(1, ncol):
         pl.semaphore_signal(barrier, inc=1, device_id={"col": (x + d) % ncol}, device_id_type=MESH)
     ends = jnp.where(z > 0, 1, 0) + jnp.where(z < nz - 1, 1, 0)
-    pl.semaphore_wait(barrier, nout + ncol - 2 + ends)
+    pl.semaphore_wait(barrier, ncol + 1 + ends)
 
     def slots(oo, zz, count, cols):
         start = pl.multiple_of((oo * nz + zz) * tg, tg)
@@ -136,9 +133,11 @@
             to_y(g_ref, z, full, g_send, gy_recv.at[z]).start()
         near(own, z, c).start()
 
-    def a_first(d):
-        target = (o + d) % nout
-        return remote(a_ref.at[target], av.at[o * ncol + x], a_send, a1_recv.at[d - 1], {"outer": target})
+    def a_got(source, target):
+        return a1_recv.at[(target - source + nout) % nout - 1]
+
+    def a_first(target):
+        return remote(a_ref.at[target], av.at[o * ncol + x], a_send, a_got(o, target), {"outer": target})
 
     def a_second(oo, d, own=False):
         k = oo * ncol + x
@@ -154,7 +153,7 @@
 
     def pass_on(oo):
         k = oo * ncol + x
-        remote(av.at[k], av.at[k], a_send, a1_recv.at[(o - oo + nout) % nout - 1], {"outer": oy}).wait_recv()
+        remote(av.at[k], av.at[k], a_send, a_got(oo, o), {"outer": oy}).wait_recv()
         for d in range(1, ncol):
             a_second(oo, d).start()
 
@@ -247,6 +246,8 @@
         if s == nz - 1:
             local_g.wait()
             local_a.wait()
+            load_rm.start()
+            load_cm.start()
             settle(av.at[pl.ds(0, (ncol - 1) * nout)], a2_recv)
         for c in range(len(chain)):
             @pl.when(z - s >= 0)
@@ -268,11 +269,14 @@
                 relay(z + s, c, onward)
 
             if s == 1 and c == 0:
-                for d in range(1, nout):
-                    a_first(d).start()
+                a_first(op).start()
+                a_first(oy).start()
                 for d in range(1, ncol):
                     a_second(o, d, True).start()
                 local_a.start()
+            if s == 1 and c == 1:
+                pass_on(op)
+                a_first(od).start()
             if s == nz - 1:
                 first_half(c)
                 if c == len(chain) - 2:
@@ -281,7 +285,6 @@
 
         if s == 1:
             take_whole(z)
-            pass_on(op)
         if s == min(2, nz - 1):
             for c in range(2):
                 pass_on((1 - y) * 2 + c)
@@ -397,11 +400,12 @@
     arrived = jnp.sum(late[...], axis=0)
     new_late = decay * cm[:, wide:] + (1.0 - decay) * arrived[:, :rest] / D
     nc_ref[:, wide:] = new_late
+    roots = [lax.rsqrt(new_early), lax.rsqrt(new_late)]
     settle(others, o_sem.at[1])
     total = jnp.sum(arrived[:, rest:] + jnp.sum(others[...], axis=0), axis=1, keepdims=True)
-    factor = D / total
-    bycol_ref[:, :wide] = lax.rsqrt(new_early * factor)
-    bycol_ref[:, wide:] = lax.rsqrt(new_late * factor)
+    root = lax.rsqrt(D / total)
+    bycol_ref[:, :wide] = roots[0] * root
+    bycol_ref[:, wide:] = roots[1] * root
 
     at_end = (z == 0) | (z == nz - 1)
 
@@ -487,7 +491,7 @@
             dma(()),
             dma(()),
             dma(()),
-            dma((4,)),
+            dma((2,)),
             dma((2,)), dma((2,)), dma((2,)), dma((2,)), dma((2,)),
             pltpu.SemaphoreType.REGULAR,
         ],

time: 102 us -> 103 us (level)
  no operation moved by 1% of the time
where the time goes in v4:
time: 103 us; the launch traced here: 102 us
  Pallas kernels  102 us (99%)
    pallas_call x1, Pallas kernels, body(): pl.pallas_call(functools.partial(kernel, nout, nz, ncol, 1.0 / tokens **...  99.4 us
    pallas_call x1, Pallas kernels, body(): pl.pallas_call(functools.partial(update_kernel, rows // parts), out_shape...  2.37 us

profile of v4, /device:TPU:0, one launch (start us, length us, event | category | flops | bytes accessed | tf_op | source)
XLA Modules:
  0.0 102.4 jit_solution(18351438357427143700)
XLA Ops:
  0.6 99.4 %shard_map.67 = (f32[576,4096]{1,0:T(8,128)S(1)}, f32[1,576]{1,0:T(1,128)S(1)}, f32[576,128]{1,0:T(8,128)S(1)}, f32[1,4096]{1,0:T(1,128)S(1)}, f32[1,4096]{1,0:T(1,128)S(1)}) custom-call(bf16[256,2304]{1,0:T(8,128)(2,1)} %raw_ref.1, bf16[128,4096]{1,0:T(8,128)(2,1)} %g_ref.1, f32[576]{0:T(1024)} %rm_hbm.1, f32[4096]{0:T(1024)} %cm_hbm.1), custom_call_target="tpu_custom_call" | custom-call | tf_op jit(solution)/shard_map/pallas_call | solution.py:459
  100.0 2.4 %shard_map.68 = (bf16[576,4096]{1,0:T(8,128)(2,1)}, f32[576]{0:T(1024)}, f32[4096]{0:T(1024)}) custom-call(f32[576,4096]{1,0:T(8,128)S(1)} %get-tuple-element.8.grad_ref, f32[576,128]{1,0:T(8,128)S(1)} %get-tuple-element.9.byrow_ref, f32[1,4096]{1,0:T(1,128)S(1)} %get-tuple-element.10.bycol_ref, f32[1,576]{1,0:T(1,128)S(1)} %get-tuple-element.11.nr_ref, ...), custom_call_target="tpu_custom_call" | custom-call | tf_op jit(solution)/shard_map/pallas_call | solution.py:508

commit v5 on v4

--- a/solution.py
+++ b/solution.py
@@ -15,7 +15,7 @@
 
 def cuts(width):
     unit = width // 128
-    share, *edges = [unit * e // 32 * 128 for e in (7, 8, 16, 24, 30, 32)]
+    share, *edges = [unit * e // 32 * 128 for e in (7, 8, 16, 24, 28, 32)]
     fine = [(a, b - a) for a, b in zip([0] + edges[:-1], edges)]
     chain = [[0, 1], [2], [3, 4]]
     by_y = (0, share)
@@ -65,7 +65,17 @@
     def settle(ref, sem):
         pltpu.make_async_copy(ref, ref, sem).wait()
 
+    def slots(oo, zz, count, cols):
+        start = pl.multiple_of((oo * nz + zz) * tg, tg)
+        return gs.at[pl.ds(start, count * tg), pl.ds(*cols)]
+
+    def place(oo, zz, cols):
+        return slots(oo, zz, 1, cols)
+
+    full = (0, width)
+    local_g = pltpu.make_async_copy(g_ref, slots(o, z, 1, full), loc_sem.at[0])
     load_a = pltpu.make_async_copy(raw_ref, raw, loc_sem.at[1])
+    local_g.start()
     load_a.start()
     load_rm = pltpu.make_async_copy(rm_hbm, rm_ref, loc_sem.at[0])
     load_cm = pltpu.make_async_copy(cm_hbm, cm_ref, loc_sem.at[1])
@@ -86,19 +96,10 @@
     ends = jnp.where(z > 0, 1, 0) + jnp.where(z < nz - 1, 1, 0)
     pl.semaphore_wait(barrier, ncol + 1 + ends)
 
-    def slots(oo, zz, count, cols):
-        start = pl.multiple_of((oo * nz + zz) * tg, tg)
-        return gs.at[pl.ds(start, count * tg), pl.ds(*cols)]
-
-    def place(oo, zz, cols):
-        return slots(oo, zz, 1, cols)
-
     def merged(c):
         first, end = fine[chain[c][0]], fine[chain[c][-1]]
         return (first[0], end[0] + end[1] - first[0])
 
-    full = (0, width)
-
     def from_z(zz, c, at):
         return gz_recv.at[(zz - at - 1 + 2 * nz) % nz, c]
 
@@ -118,8 +119,9 @@
         here = place(oy, zz, cols)
         return remote(here, here, p_send, od_recv.at[h], {"outer": op})
 
+    local_g.wait()
     for c in range(len(chain)):
-        own = g_ref.at[:, pl.ds(*merged(c))]
+        own = place(o, z, merged(c))
 
         @pl.when(z < nz - 1)
         def _():
@@ -130,7 +132,7 @@
             to_down(own, z, c).start()
 
         if c == 0:
-            to_y(g_ref, z, full, g_send, gy_recv.at[z]).start()
+            to_y(place(o, z, full), z, full, g_send, gy_recv.at[z]).start()
         near(own, z, c).start()
 
     def a_got(source, target):
@@ -143,9 +145,7 @@
         k = oo * ncol + x
         return remote(a_ref.at[o] if own else av.at[k], av.at[k], a_send, a2_recv, {"col": (x + d) % ncol})
 
-    local_g = pltpu.make_async_copy(g_ref, slots(o, z, 1, full), loc_sem.at[0])
     local_a = pltpu.make_async_copy(a_ref.at[o], av.at[o * ncol + x], loc_sem.at[1])
-    local_g.start()
     load_a.wait()
     turned = jnp.transpose(raw[...])
     for k in range(nout):
@@ -244,7 +244,6 @@
 
     for s in range(1, nz):
         if s == nz - 1:
-            local_g.wait()
             local_a.wait()
             load_rm.start()
             load_cm.start()

time: 103 us -> 101 us (0.981)
    pallas_call x1, Pallas kernels: 99.4 us -> 98.3 us  [body(): pl.pallas_call(functools.partial(kernel, nout, nz, ncol, 1.0 / tokens **...]
where the time goes in v5:
time: 101 us
  Pallas kernels  101 us (100%)
    pallas_call x1, Pallas kernels, body(): pl.pallas_call(functools.partial(kernel, nout, nz, ncol, 1.0 / tokens **...  98.3 us
    pallas_call x1, Pallas kernels, body(): pl.pallas_call(functools.partial(update_kernel, rows // parts), out_shape...  2.37 us

profile of v5, /device:TPU:0, one launch (start us, length us, event | category | flops | bytes accessed | tf_op | source)
XLA Modules:
  0.0 101.3 jit_solution(7586897831209720111)
XLA Ops:
  0.6 98.3 %shard_map.67 = (f32[576,4096]{1,0:T(8,128)S(1)}, f32[1,576]{1,0:T(1,128)S(1)}, f32[576,128]{1,0:T(8,128)S(1)}, f32[1,4096]{1,0:T(1,128)S(1)}, f32[1,4096]{1,0:T(1,128)S(1)}) custom-call(bf16[256,2304]{1,0:T(8,128)(2,1)} %raw_ref.1, bf16[128,4096]{1,0:T(8,128)(2,1)} %g_ref.1, f32[576]{0:T(1024)} %rm_hbm.1, f32[4096]{0:T(1024)} %cm_hbm.1), custom_call_target="tpu_custom_call" | custom-call | tf_op jit(solution)/shard_map/pallas_call | solution.py:458
  98.9 2.4 %shard_map.68 = (bf16[576,4096]{1,0:T(8,128)(2,1)}, f32[576]{0:T(1024)}, f32[4096]{0:T(1024)}) custom-call(f32[576,4096]{1,0:T(8,128)S(1)} %get-tuple-element.8.grad_ref, f32[576,128]{1,0:T(8,128)S(1)} %get-tuple-element.9.byrow_ref, f32[1,4096]{1,0:T(1,128)S(1)} %get-tuple-element.10.bycol_ref, f32[1,576]{1,0:T(1,128)S(1)} %get-tuple-element.11.nr_ref, ...), custom_call_target="tpu_custom_call" | custom-call | tf_op jit(solution)/shard_map/pallas_call | solution.py:507

commit v6 on v5

--- a/solution.py
+++ b/solution.py
@@ -17,10 +17,14 @@
     unit = width // 128
     share, *edges = [unit * e // 32 * 128 for e in (7, 8, 16, 24, 28, 32)]
     fine = [(a, b - a) for a, b in zip([0] + edges[:-1], edges)]
-    chain = [[0, 1], [2], [3, 4]]
+    chain = [[0, 1], [2, 3, 4]]
     by_y = (0, share)
-    by_z = [(share, edges[0] - share)] + fine[1:]
-    return fine, chain, by_y, by_z
+    start, size = fine[-1]
+    head = max(size // 256, 1) * 128
+    lasts = [(start, head), (start + head, size - head)] if size > head else [(start, size)]
+    subs = [[cols] for cols in fine[:-1]] + [lasts]
+    by_z = [[(share, edges[0] - share)]] + subs[1:]
+    return fine, chain, by_y, by_z, subs
 
 
 def each(first, last, f):
@@ -36,13 +40,13 @@
     raw_ref, g_ref, rm_hbm, cm_hbm,
     acc, nr_ref, byrow_ref, nc_ref, bycol_ref,
     gs, av, raw, a_ref, rm_ref, cm_ref, rowp, early, earlyz, late, others, rowbuf,
-    gz_recv, gy_recv, far_recv, mate_recv, op_recv, od_recv, a1_recv, a2_recv,
+    gz_recv, gy_recv, last_recv, op_recv, od_recv, a1_recv, a2_recv,
     g_send, p_send, a_send, loc_sem,
     e_sem, ez_sem, l_sem, o_sem, r_sem, ready,
 ):
     tg, width = g_ref.shape
     rows, ta = av.shape[1], av.shape[2]
-    fine, chain, by_y, by_z = cuts(width)
+    fine, chain, by_y, by_z, subs = cuts(width)
     last = len(fine) - 1
     wide = early.shape[2]
     o = lax.axis_index("outer")
@@ -167,10 +171,11 @@
             over(zz, fine[h], h).start()
 
     def take(h):
-        landed(end, fine[h], far_recv.at[h])
-        over(end, fine[h], h).start()
-        landed(mate, fine[h], mate_recv.at[h])
-        over(mate, fine[h], h).start()
+        for i, cols in enumerate(subs[h]):
+            both = slots(oy, 0, 2, cols)
+            remote(both, both, g_send, last_recv.at[h + i], {"outer": oy}).wait_recv()
+            over(end, cols, h).start()
+            over(mate, cols, h).start()
 
     def relay(zz, c, onward):
         here = place(o, zz, merged(c))
@@ -184,26 +189,28 @@
         @pl.when(zz == end)
         def _():
             for j in chain[c]:
-                to_y(place(o, zz, fine[j]), zz, fine[j], g_send, far_recv.at[j]).start()
+                for i, cols in enumerate(subs[j]):
+                    to_y(place(o, zz, cols), zz, cols, g_send, last_recv.at[j + i]).start()
 
         if c == 0:
             @pl.when(zz == mate)
             def _():
-                to_y(place(o, zz, by_y), zz, by_y, g_send, mate_recv.at[0]).start()
+                to_y(place(o, zz, by_y), zz, by_y, g_send, last_recv.at[0]).start()
 
         near(here, zz, c).start()
 
     def extra():
         for h in range(len(fine)):
-            here = place(oy, z, by_z[h])
-
-            @pl.when(mate > z)
-            def _():
-                remote(here, here, g_send, mate_recv.at[h], up).start()
-
-            @pl.when(mate < z)
-            def _():
-                remote(here, here, g_send, mate_recv.at[h], down).start()
+            for i, cols in enumerate(by_z[h]):
+                here = place(oy, z, cols)
+
+                @pl.when(mate > z)
+                def _():
+                    remote(here, here, g_send, last_recv.at[h + i], up).start()
+
+                @pl.when(mate < z)
+                def _():
+                    remote(here, here, g_send, last_recv.at[h + i], down).start()
 
     def dots(oo, cols):
         total = None
@@ -273,7 +280,6 @@
                 for d in range(1, ncol):
                     a_second(o, d, True).start()
                 local_a.start()
-            if s == 1 and c == 1:
                 pass_on(op)
                 a_first(od).start()
             if s == nz - 1:
@@ -425,8 +431,8 @@
     settle(rowbuf.at[pl.ds(1, ncol - 1)], r_sem.at[0])
 
 
-def update_kernel(step, grad_ref, byrow_ref, bycol_ref, nr_ref, nc_ref, out_hbm, row_hbm, col_hbm, out, row, col, sem):
-    parts = out.shape[0] // step
+def update_kernel(edges, grad_ref, byrow_ref, bycol_ref, nr_ref, nc_ref, out_hbm, row_hbm, col_hbm, out, row, col, sem):
+    parts = len(edges) - 1
     row[...] = nr_ref[...].reshape(row.shape)
     col[...] = nc_ref[...].reshape(col.shape)
     copies = [
@@ -436,7 +442,7 @@
     for c in copies:
         c.start()
     for k in range(parts):
-        here = pl.ds(k * step, step)
+        here = pl.ds(edges[k], edges[k + 1] - edges[k])
         out[here, :] = (grad_ref[here, :] * jnp.tile(byrow_ref[here, :], (1, out.shape[1] // 128)) * bycol_ref[...]).astype(out.dtype)
         copies.append(pltpu.make_async_copy(out.at[here], out_hbm.at[here], sem.at[k]))
         copies[-1].start()
@@ -453,7 +459,7 @@
     vmem = pl.BlockSpec(memory_space=pltpu.VMEM)
     hbm = pl.BlockSpec(memory_space=pl.ANY)
     dma = pltpu.SemaphoreType.DMA
-    fine, chain, _, _ = cuts(width)
+    fine, chain, _, _, subs = cuts(width)
     wide = fine[2][0] + fine[2][1]
     grad, new_row, by_row, new_col, by_col = pl.pallas_call(
         functools.partial(kernel, nout, nz, ncol, 1.0 / tokens**0.5, decay),
@@ -481,8 +487,7 @@
             pltpu.VMEM((ncol, 1, rows), f32),
             dma((nz - 1, len(chain))),
             dma((nz,)),
-            dma((len(fine),)),
-            dma((len(fine),)),
+            dma((sum(map(len, subs)),)),
             dma((len(chain),)),
             dma((len(fine),)),
             dma((nout - 1,)),
@@ -503,9 +508,9 @@
         pltpu.with_memory_space_constraint(row_moment, pltpu.HBM),
         pltpu.with_memory_space_constraint(col_moment, pltpu.HBM),
     )
-    parts = next(n for n in (9, 6, 4, 3, 2, 1) if n == 1 or rows % (n * 16) == 0)
+    edges = [0, 16, 64, *range(192, rows + 1, 128)] if rows % 64 == 0 else [0, rows]
     return pl.pallas_call(
-        functools.partial(update_kernel, rows // parts),
+        functools.partial(update_kernel, edges),
         out_shape=(
             jax.ShapeDtypeStruct((rows, width), bf16),
             jax.ShapeDtypeStruct((rows,), f32),
@@ -517,7 +522,7 @@
             pltpu.VMEM((rows, width), bf16),
             pltpu.VMEM((rows,), f32),
             pltpu.VMEM((width,), f32),
-            dma((parts + 2,)),
+            dma((len(edges) + 1,)),
         ],
         compiler_params=pltpu.CompilerParams(vmem_limit_bytes=24 * 1024 * 1024),
     )(grad, by_row, by_col, new_row, new_col)

time: 101 us -> 101 us (level)
  no operation moved by 1% of the time
where the time goes in v6:
time: 101 us
  Pallas kernels  100 us (99%)
    pallas_call x1, Pallas kernels, body(): pl.pallas_call(functools.partial(kernel, nout, nz, ncol, 1.0 / tokens **...  98 us
    pallas_call x1, Pallas kernels, body(): pl.pallas_call(functools.partial(update_kernel, edges), out_shape=(jax.Sh...  2.36 us

profile of v6, /device:TPU:0, one launch (start us, length us, event | category | flops | bytes accessed | tf_op | source)
XLA Modules:
  0.0 101.0 jit_solution(14594335417507036887)
XLA Ops:
  0.6 98.0 %shard_map.67 = (f32[576,4096]{1,0:T(8,128)S(1)}, f32[1,576]{1,0:T(1,128)S(1)}, f32[576,128]{1,0:T(8,128)S(1)}, f32[1,4096]{1,0:T(1,128)S(1)}, f32[1,4096]{1,0:T(1,128)S(1)}) custom-call(bf16[256,2304]{1,0:T(8,128)(2,1)} %raw_ref.1, bf16[128,4096]{1,0:T(8,128)(2,1)} %g_ref.1, f32[576]{0:T(1024)} %rm_hbm.1, f32[4096]{0:T(1024)} %cm_hbm.1), custom_call_target="tpu_custom_call" | custom-call | tf_op jit(solution)/shard_map/pallas_call | solution.py:464
  98.6 2.4 %shard_map.68 = (bf16[576,4096]{1,0:T(8,128)(2,1)}, f32[576]{0:T(1024)}, f32[4096]{0:T(1024)}) custom-call(f32[576,4096]{1,0:T(8,128)S(1)} %get-tuple-element.8.grad_ref, f32[576,128]{1,0:T(8,128)S(1)} %get-tuple-element.9.byrow_ref, f32[1,4096]{1,0:T(1,128)S(1)} %get-tuple-element.10.bycol_ref, f32[1,576]{1,0:T(1,128)S(1)} %get-tuple-element.11.nr_ref, ...), custom_call_target="tpu_custom_call" | custom-call | tf_op jit(solution)/shard_map/pallas_call | solution.py:512

commit v7 on v6

--- a/solution.py
+++ b/solution.py
@@ -315,7 +315,7 @@
         def one(offset, tile):
             cols = pl.ds(pl.multiple_of(begin + offset, 128), tile)
             there = pl.ds(pl.multiple_of(begin - shift + offset, 128), tile)
-            grad = (acc[:, cols] + dots(od, cols)) * scale if split else (acc[:, cols] + (dots(oy, cols) + dots(od, cols))) * scale
+            grad = acc[:, cols] + (dots(od, cols) if split else dots(oy, cols) + dots(od, cols))
             acc[:, cols] = grad
             squares = grad * grad
             part = squares[:, :128]
@@ -360,6 +360,7 @@
             for d in range(1, ncol):
                 pl.semaphore_signal(ready, inc=1, device_id={"col": (x + d) % ncol}, device_id_type=MESH)
 
+    weight = (1.0 - decay) * scale * scale
     group = nout * nz
     rest = width - wide
 
@@ -372,7 +373,7 @@
     def send_late(k):
         remote(late.at[0], late.at[mirror(k)], l_sem.at[0], l_sem.at[1], peer(k, 0)).start()
 
-    late[0, :, pl.ds(rest, 128)] = jnp.sum(rowp[...], axis=0, keepdims=True) * ((1.0 - decay) / F) + old_share
+    late[0, :, pl.ds(rest, 128)] = jnp.sum(rowp[...], axis=0, keepdims=True) * (weight / F) + old_share
     pl.semaphore_wait(ready, ncol - 1)
     for d in range(1, ncol):
         def send_other(k):
@@ -381,29 +382,29 @@
 
         each(0, group, send_other)
     each(1, group, send_late)
+    rowbuf[0] = jnp.sum(jnp.transpose(rowp[...]), axis=0, keepdims=True)
+
+    def r_first(d):
+        return remote(rowbuf.at[0], rowbuf.at[ncol - d], r_sem.at[0], r_sem.at[1], {"col": (x + d) % ncol})
+
+    for d in range(1, ncol):
+        r_first(d).start()
     settle(early.at[pl.ds(1, nout - 1)], e_sem.at[1])
     earlyz[0] = jnp.sum(early[...], axis=0)
     for d in range(1, nz):
         e_second(d).start()
-    rowbuf[0] = jnp.sum(jnp.transpose(rowp[...]), axis=0, keepdims=True)
-
-    def r_first(d):
-        return remote(rowbuf.at[0], rowbuf.at[ncol - d], r_sem.at[0], r_sem.at[1], {"col": (x + d) % ncol})
-
-    for d in range(1, ncol):
-        r_first(d).start()
     settle(rowbuf.at[pl.ds(1, ncol - 1)], r_sem.at[1])
     row_sq = jnp.sum(rowbuf[...], axis=0)
-    new_row = decay * old + (1.0 - decay) * row_sq / F
+    new_row = decay * old + weight * row_sq / F
     nr_ref[...] = new_row
-    byrow_ref[...] = jnp.transpose(jnp.broadcast_to(lax.rsqrt(new_row), (128, rows)))
+    byrow_ref[...] = jnp.transpose(jnp.broadcast_to(lax.rsqrt(new_row) * scale, (128, rows)))
     settle(earlyz.at[pl.ds(1, nz - 1)], ez_sem.at[1])
     cm = cm_ref[...].reshape(1, width)
-    new_early = decay * cm[:, :wide] + (1.0 - decay) * jnp.sum(earlyz[...], axis=0) / D
+    new_early = decay * cm[:, :wide] + weight * jnp.sum(earlyz[...], axis=0) / D
     nc_ref[:, :wide] = new_early
     settle(late.at[pl.ds(1, group - 1)], l_sem.at[1])
     arrived = jnp.sum(late[...], axis=0)
-    new_late = decay * cm[:, wide:] + (1.0 - decay) * arrived[:, :rest] / D
+    new_late = decay * cm[:, wide:] + weight * arrived[:, :rest] / D
     nc_ref[:, wide:] = new_late
     roots = [lax.rsqrt(new_early), lax.rsqrt(new_late)]
     settle(others, o_sem.at[1])

time: 101 us -> 101 us (level)
  no operation moved by 1% of the time
where the time goes in v7:
time: 101 us
  Pallas kernels  100 us (99%)
    pallas_call x1, Pallas kernels, body(): pl.pallas_call(functools.partial(kernel, nout, nz, ncol, 1.0 / tokens **...  98 us
    pallas_call x1, Pallas kernels, body(): pl.pallas_call(functools.partial(update_kernel, edges), out_shape=(jax.Sh...  2.36 us

profile of v7, /device:TPU:0, one launch (start us, length us, event | category | flops | bytes accessed | tf_op | source)
XLA Modules:
  0.0 101.0 jit_solution(9141818406016933283)
XLA Ops:
  0.6 98.0 %shard_map.67 = (f32[576,4096]{1,0:T(8,128)S(1)}, f32[1,576]{1,0:T(1,128)S(1)}, f32[576,128]{1,0:T(8,128)S(1)}, f32[1,4096]{1,0:T(1,128)S(1)}, f32[1,4096]{1,0:T(1,128)S(1)}) custom-call(bf16[256,2304]{1,0:T(8,128)(2,1)} %raw_ref.1, bf16[128,4096]{1,0:T(8,128)(2,1)} %g_ref.1, f32[576]{0:T(1024)} %rm_hbm.1, f32[4096]{0:T(1024)} %cm_hbm.1), custom_call_target="tpu_custom_call" | custom-call | tf_op jit(solution)/shard_map/pallas_call | solution.py:465
  98.6 2.4 %shard_map.68 = (bf16[576,4096]{1,0:T(8,128)(2,1)}, f32[576]{0:T(1024)}, f32[4096]{0:T(1024)}) custom-call(f32[576,4096]{1,0:T(8,128)S(1)} %get-tuple-element.8.grad_ref, f32[576,128]{1,0:T(8,128)S(1)} %get-tuple-element.9.byrow_ref, f32[1,4096]{1,0:T(1,128)S(1)} %get-tuple-element.10.bycol_ref, f32[1,576]{1,0:T(1,128)S(1)} %get-tuple-element.11.nr_ref, ...), custom_call_target="tpu_custom_call" | custom-call | tf_op jit(solution)/shard_map/pallas_call | solution.py:513
